TPU v7x, 32 devices: a whole 2x2x4 slice. The times are simulated.
32 devices in a mesh: grp: 2 (over x), tile: 16 (over z, y, core).
Axes of the slice: x: 2, y: 2, z: 4, core: 2. Of those that a mesh axis runs over, the one named last changes fastest.
Arguments:
- site_cell: int32 [2048, 2], P(('grp', 'tile')), may hold values from 0 to 63
- site_power: float32 [2048], P(('grp', 'tile')), may hold values from -4.5 to -2
- site_tile: int32 [2048, 1], P(('grp', 'tile')), may hold values from 0 to 15; in each aligned block of 64 rows (0 to 63, 64 to 127, ...) at most 8 rows name the same one
- shadow: bfloat16 [2048, 4096], P(('grp', 'tile')), may hold values from -3.75 to 3.75
Outputs:
- count_dist: float32 [16, 8, 4096], P('tile', None, 'grp')
Inputs may be any that keep to these rules, and one draw needn't show every extreme that they name: `site_tile`: among the 64 sites of one device (aligned blocks of rows), at most 8 name the same tile; in some devices a tile is named by exactly 8.
All inputs are finite; a program needn't handle non-finite values.
Results may differ from a plain program's by a relative error of at most 0.00075.
Values may be sent and summed in bfloat16 or wider, within the bound.
No kernel may reach another device: no remote copies, remote signals or barrier semaphores. Data moves between devices by JAX's collectives and lax.ppermute only.
A program may use at most 64 MiB of HBM per device.

v0:
```python
import jax
import jax.numpy as jnp
from jax import lax
from jax.sharding import PartitionSpec as P

WIN = 64
KMAX = 8
reach_sq = 16.0


def joined(value, axis, join):
    pieces = lax.all_gather(value, axis)
    head = pieces[0]
    tail = pieces[1:]
    so_far, _ = lax.scan(lambda so_far, piece: (join(so_far, piece), None), head, tail)
    return so_far


def convolve(first_dist, second_dist, state_axis):
    count_first = first_dist.shape[state_axis]
    count_second = second_dist.shape[state_axis]
    count_out = min(count_first + count_second - 1, KMAX)
    term_list = []
    for k in range(count_out):
        running = None
        for i in range(max(0, k - count_second + 1), min(k, count_first - 1) + 1):
            product = lax.index_in_dim(
                first_dist, i, state_axis, keepdims=False
            ) * lax.index_in_dim(second_dist, k - i, state_axis, keepdims=False)
            running = product if running is None else running + product
        term_list.append(running)
    return jnp.stack(term_list, state_axis)


def merge_pair(first_dist, second_dist):
    return convolve(first_dist, second_dist, 0)


def fold_slots(slot_probs):
    detect_prob = slot_probs.astype(jnp.float32)
    states = jnp.stack([1.0 - detect_prob, detect_prob], axis=1)
    while states.shape[0] > 1:
        if states.shape[0] % 2:
            count_states = states.shape[1]
            columns = states.shape[2]
            identity = jnp.concatenate(
                [
                    jnp.ones((1, 1, columns), jnp.float32),
                    jnp.zeros((1, count_states - 1, columns), jnp.float32),
                ],
                axis=1,
            )
            states = jnp.concatenate([states, identity], axis=0)
        states = convolve(states[0::2], states[1::2], 1)
    result = states[0]
    if result.shape[0] < KMAX:
        result = jnp.concatenate(
            [result, jnp.zeros((KMAX - result.shape[0], result.shape[1]), jnp.float32)], axis=0
        )
    return result


def fold_columns(slot_probs, block_width):
    slots, columns = slot_probs.shape
    blocks = slot_probs.reshape(slots, columns // block_width, block_width).transpose(1, 0, 2)
    folded = lax.map(fold_slots, blocks)
    return folded.transpose(1, 0, 2).reshape(KMAX, columns)


def site_probs(site_cell, site_power, shadow):
    cell_index = jnp.arange(shadow.shape[1], dtype=jnp.int32)
    cell_row = (cell_index // WIN).astype(jnp.float32)
    cell_col = (cell_index % WIN).astype(jnp.float32)
    row_gap = cell_row[None, :] - site_cell[:, 0:1].astype(jnp.float32)
    col_gap = cell_col[None, :] - site_cell[:, 1:2].astype(jnp.float32)
    margin = (
        site_power[:, None]
        - jnp.log(1.0 + (row_gap * row_gap + col_gap * col_gap) / reach_sq)
        + shadow.astype(jnp.float32)
    )
    return jax.nn.sigmoid(margin).astype(jnp.bfloat16)


def on_device(site_cell, site_power, site_tile, shadow):
    tiles = lax.axis_size("tile")
    groups = lax.axis_size("grp")
    site_count = shadow.shape[0]
    capacity = max(2, 2 * site_count // tiles)
    cells_all = shadow.shape[1]
    width = cells_all // groups
    detect_prob = site_probs(site_cell, site_power, shadow)
    owner_tile = site_tile[:, 0]
    hit_table = (owner_tile[:, None] == jnp.arange(tiles, dtype=jnp.int32)[None, :]).astype(
        jnp.int32
    )
    slot_rank = jnp.sum((jnp.cumsum(hit_table, axis=0) - hit_table) * hit_table, axis=1)
    slot_index = owner_tile * capacity + slot_rank
    selector = (
        slot_index[None, :] == jnp.arange(tiles * capacity, dtype=jnp.int32)[:, None]
    ).astype(jnp.bfloat16)
    outgoing = jnp.dot(selector, detect_prob, preferred_element_type=jnp.float32).astype(
        jnp.bfloat16
    )
    outgoing = outgoing.reshape(tiles * capacity, groups, width)
    items = jnp.moveaxis(
        lax.all_to_all(outgoing, "tile", split_axis=0, concat_axis=0, tiled=True), 1, 0
    )
    folded = lax.map(lambda piece: fold_columns(piece, min(piece.shape[1], 512)), items)
    group_dist = jnp.moveaxis(folded, 0, 1)
    merged = joined(group_dist, "grp", merge_pair)
    own_states = lax.dynamic_index_in_dim(merged, lax.axis_index("grp"), 1, keepdims=False)
    return own_states[None, :, :]


def solution(mesh):
    placed = (
        P(("grp", "tile"), None),
        P(("grp", "tile")),
        P(("grp", "tile"), None),
        P(("grp", "tile"), None),
    )
    return jax.shard_map(
        on_device, mesh=mesh, in_specs=placed, out_specs=P("tile", None, "grp"), check_vma=False
    )
```

profile of v0, /device:TPU:11, one launch (start us, length us, event | category | flops | bytes accessed | tf_op | source)
XLA Modules:
  0.0 92.0 jit_solution(106595305176104086)
XLA Ops:
  0.0 0.7 fusion.24
  0.8 0.8 select_reduce_fusion
  1.7 0.7 multiply_add_fusion.35
  2.3 0.8 convert_bitcast_fusion.1
  3.1 2.0 %convolution_convert_fusion = bf16[128,4096]{1,0:T(8,128)(2,1)S(1)} fusion(bf16[64,4096]{1,0:T(8,128)(2,1)} %param.11, f32[64]{0:T(128)S(1)} %get-tuple-element.135, f32[4096]{0:T(1024)S(1)} %get-tuple-element.137, f32[64]{0:T(128)S(1)} %get-tuple-element.134, f32[4096]{0:T(1024)S(1)} %get-tuple-element.136, f32[64]{0:T(128)} %param.9, ...), kind=kOutput, calls=%fused_computation.71 | convolution fusion | flops 71311360 | bytes 1606656 | tf_op jit(solution)/shard_map/dot_general | solution.py:101
  5.1 1.6 %reshape.1052 = bf16[128,2,2048]{2,1,0:T(2,128)(2,1)} reshape(bf16[128,4096]{1,0:T(8,128)(2,1)S(1)} %convolution_convert_fusion) | data formatting | bytes 2097152 | tf_op jit(solution)/shard_map/reshape | solution.py:104
  6.7 6.6 %all-to-all-start = ((bf16[128,2,2048]{2,1,0:T(2,128)(2,1)}), bf16[128,2,2048]{2,1,0:T(2,128)(2,1)S(1)}, u32[]{:S(2)}, u32[]{:S(2)}) async-start(bf16[128,2,2048]{2,1,0:T(2,128)(2,1)} %reshape.1052), calls=%async_computation | async-start | bytes 2097152 | tf_op jit(solution)/shard_map/all_to_all | solution.py:106
  13.3 24.8 %all-to-all-done = bf16[128,2,2048]{2,1,0:T(2,128)(2,1)S(1)} async-done(((bf16[128,2,2048]{2,1,0:T(2,128)(2,1)}), bf16[128,2,2048]{2,1,0:T(2,128)(2,1)S(1)}, u32[]{:S(2)}, u32[]{:S(2)}) %all-to-all-start) | async-done | bytes 1048608 | tf_op jit(solution)/shard_map/all_to_all | solution.py:106
  38.5 45.9 %while.25 = (s32[]{:T(128)}, f32[2,8,2048]{2,1,0:T(8,128)S(1)}, bf16[2,128,2048]{2,1,0:T(8,128)(2,1)S(1)}, s32[]{:T(128)}, s32[]{:T(128)}, /*index=5*/s32[]{:T(128)}) while((s32[]{:T(128)}, f32[2,8,2048]{2,1,0:T(8,128)S(1)}, bf16[2,128,2048]{2,1,0:T(8,128)(2,1)S(1)}, s32[]{:T(128)}, s32[]{:T(128)}, /*index=5*/s32[]{:T(128)}) %tuple.136), condition=%wide.region_5.6_spmd, body=%wide.region_2.5_spmd.sunk | while | flops 1654788 | bytes 14295218 | solution.py:108
  38.6 0.4 reshape.1066
  39.0 22.5 %while.26 = (s32[]{:T(128)}, f32[4,8,512]{2,1,0:T(8,128)S(1)}, bf16[4,128,512]{2,0,1:T(4,128)(2,1)S(1)}, s32[]{:T(128)}) while((s32[]{:T(128)}, f32[4,8,512]{2,1,0:T(8,128)S(1)}, bf16[4,128,512]{2,0,1:T(4,128)(2,1)S(1)}, s32[]{:T(128)}) %tuple.139), condition=%wide.region_4.4_spmd, body=%wide.region_3.3_spmd.sunk | while | flops 1654786 | bytes 12066877 | solution.py:66
  39.0 0.4 broadcast_subtract_fusion.2
  39.4 0.5 pad_maximum_fusion.4
  41.1 0.5 stack.31
  42.4 0.4 stack.32
  44.6 0.4 broadcast_subtract_fusion.2
  45.0 0.5 pad_maximum_fusion.4
  46.7 0.5 stack.31
  48.0 0.4 stack.32
  50.2 0.4 broadcast_subtract_fusion.2
  50.6 0.5 pad_maximum_fusion.4
  51.9 0.4 slice_multiply_fusion.20
  52.3 0.5 stack.31
  53.6 0.4 stack.32
  55.9 0.4 broadcast_subtract_fusion.2
  56.2 0.5 pad_maximum_fusion.4
  57.9 0.5 stack.31
  59.2 0.4 stack.32
  61.5 0.4 reshape.1066
  61.9 22.5 %while.26 = (s32[]{:T(128)}, f32[4,8,512]{2,1,0:T(8,128)S(1)}, bf16[4,128,512]{2,0,1:T(4,128)(2,1)S(1)}, s32[]{:T(128)}) while((s32[]{:T(128)}, f32[4,8,512]{2,1,0:T(8,128)S(1)}, bf16[4,128,512]{2,0,1:T(4,128)(2,1)S(1)}, s32[]{:T(128)}) %tuple.139), condition=%wide.region_4.4_spmd, body=%wide.region_3.3_spmd.sunk | while | flops 1654786 | bytes 12066877 | solution.py:66
  62.0 0.4 broadcast_subtract_fusion.2
  62.3 0.5 pad_maximum_fusion.4
  64.0 0.5 stack.31
  65.3 0.4 stack.32
  67.6 0.4 broadcast_subtract_fusion.2
  67.9 0.5 pad_maximum_fusion.4
  69.6 0.5 stack.31
  70.9 0.4 stack.32
  73.2 0.4 broadcast_subtract_fusion.2
  73.6 0.5 pad_maximum_fusion.4
  75.2 0.5 stack.31
  76.6 0.4 stack.32
  78.8 0.4 broadcast_subtract_fusion.2
  79.2 0.5 pad_maximum_fusion.4
  80.9 0.5 stack.31
  82.2 0.4 stack.32
  84.4 6.0 %all-gather = f32[16,2,2048]{2,0,1:T(8,128)S(1)} all-gather(f32[8,2,2048]{2,0,1:T(8,128)S(1)} %bitcast.234), channel_id=2, replica_groups=mesh['grp'=2,'tile'=16] {'grp'}, dimensions={0}, use_global_device_ids=true | all-gather | bytes 393216 | tf_op jit(solution)/shard_map/all_gather | solution.py:12
  91.3 0.6 dynamic-slice_bitcast_fusion
  (270 shorter events, 29.8 us)
Async XLA Ops:
  6.7 31.5 %all-to-all-start = ((bf16[128,2,2048]{2,1,0:T(2,128)(2,1)}), bf16[128,2,2048]{2,1,0:T(2,128)(2,1)S(1)}, u32[]{:S(2)}, u32[]{:S(2)}) async-start(bf16[128,2,2048]{2,1,0:T(2,128)(2,1)} %reshape.1052), calls=%async_computation | async-start | bytes 2097152 | tf_op jit(solution)/shard_map/all_to_all | solution.py:106
where the time goes:
time: 92.2 us; the launch traced here: 92 us
  other arithmetic  34.7 us (38%)
  waiting for transfers between devices  24.8 us (27%)
  local copies, waits for them, and re-layouts  15.6 us (17%)
  starting transfers between devices  6.61 us (7%)
  blocking collectives  5.99 us (6%)
  loops' own time  2.16 us (2%)
  matrix products  2.01 us (2%)
    all_to_all x1, waiting for transfers between devices, on_device(): lax.all_to_all(outgoing, 'tile', split_axis=0, concat_axis=0, tiled=True)  24.8 us
    add x156, other arithmetic, convolve(): running = product if running is None else running + product  16.5 us
    another operation x41, local copies, waits for them, and re-layouts, convolve(): return jnp.stack(term_list, state_axis)  10.5 us
    all_to_all x1, starting transfers between devices, on_device(): lax.all_to_all(outgoing, 'tile', split_axis=0, concat_axis=0, tiled=True)  6.61 us
    all_gather x1, blocking collectives, joined(): pieces = lax.all_gather(value, axis)  5.99 us
    mul x16, other arithmetic, convolve(): lax.index_in_dim(first_dist, i, state_axis, keepdims=False)  5.62 us
    another operation x8, other arithmetic, fold_slots(): states = jnp.stack([1.0 - detect_prob, detect_prob], axis=1)  3.81 us
    sub x8, other arithmetic, fold_slots(): states = jnp.stack([1.0 - detect_prob, detect_prob], axis=1)  2.91 us
  transfers between devices with their start and end apart: 1, of which 1 were waited for; matrix products, arithmetic and copies ran while one was open for 0% of the time, Pallas kernels for 0%

commit v1 on v0

--- a/solution.py
+++ b/solution.py
@@ -6,6 +6,22 @@
 WIN = 64
 KMAX = 8
 reach_sq = 16.0
+
+
+def swapped_with_each(x, axis, split, join):
+    ways, here = (lax.axis_size(axis), lax.axis_index(axis))
+    width = x.shape[split] // ways
+    dims = list(x.shape)
+    dims[split] = width
+    height = dims[join]
+    dims[join] = height * ways
+    full = jnp.zeros(dims, x.dtype)
+    for mask in range(ways):
+        part = lax.dynamic_slice_in_dim(x, (here ^ mask) * width, width, axis=split)
+        if mask:
+            part = lax.ppermute(part, axis, [(d, d ^ mask) for d in range(ways)])
+        full = lax.dynamic_update_slice_in_dim(full, part, (here ^ mask) * height, axis=join)
+    return full
 
 
 def joined(value, axis, join):
@@ -102,9 +118,7 @@
         jnp.bfloat16
     )
     outgoing = outgoing.reshape(tiles * capacity, groups, width)
-    items = jnp.moveaxis(
-        lax.all_to_all(outgoing, "tile", split_axis=0, concat_axis=0, tiled=True), 1, 0
-    )
+    items = jnp.moveaxis(swapped_with_each(outgoing, "tile", 0, 0), 1, 0)
     folded = lax.map(lambda piece: fold_columns(piece, min(piece.shape[1], 512)), items)
     group_dist = jnp.moveaxis(folded, 0, 1)
     merged = joined(group_dist, "grp", merge_pair)

time: 92.2 us -> 95.6 us (1.037)
  starting transfers between devices: 6.61 us -> 19.2 us
  waiting for transfers between devices: 24.8 us -> 14.7 us
    all_to_all x1 -> x0, waiting for transfers between devices: 24.8 us -> none  [on_device(): lax.all_to_all(outgoing, 'tile', split_axis=0, concat_axis=0, tiled=True)]
    ppermute x0 -> x15, starting transfers between devices: none -> 19.2 us  [swapped_with_each(): part = lax.ppermute(part, axis, [(d, d ^ mask) for d in range(ways)])]
    ppermute x0 -> x15, waiting for transfers between devices: none -> 14.7 us  [swapped_with_each(): part = lax.ppermute(part, axis, [(d, d ^ mask) for d in range(ways)])]
    all_to_all x1 -> x0, starting transfers between devices: 6.61 us -> none  [on_device(): lax.all_to_all(outgoing, 'tile', split_axis=0, concat_axis=0, tiled=True)]
    dynamic_slice x0 -> x1, local copies, waits for them, and re-layouts: none -> 1.1 us  [swapped_with_each(): part = lax.dynamic_slice_in_dim(x, (here ^ mask) * width, width, axis=split)]
  transfers between devices with their start and end apart: 1 -> 15, of which waited for: 1 -> 6; matrix products, arithmetic and copies ran while one was open for 0% -> 1% of each run, Pallas kernels for 0% -> 0%
where the time goes in v1:
time: 95.6 us; the launch traced here: 94.7 us
  other arithmetic  34.7 us (36%)
  starting transfers between devices  19.2 us (20%)
  local copies, waits for them, and re-layouts  16.2 us (17%)
  waiting for transfers between devices  14.7 us (15%)
  blocking collectives  5.36 us (6%)
  loops' own time  2.16 us (2%)
  matrix products  2.01 us (2%)
    ppermute x15, starting transfers between devices, swapped_with_each(): part = lax.ppermute(part, axis, [(d, d ^ mask) for d in range(ways)])  19.2 us
    add x156, other arithmetic, convolve(): running = product if running is None else running + product  16.5 us
    ppermute x15, waiting for transfers between devices, swapped_with_each(): part = lax.ppermute(part, axis, [(d, d ^ mask) for d in range(ways)])  14.7 us
    another operation x41, local copies, waits for them, and re-layouts, convolve(): return jnp.stack(term_list, state_axis)  10.5 us
    mul x16, other arithmetic, convolve(): lax.index_in_dim(first_dist, i, state_axis, keepdims=False)  5.62 us
    all_gather x1, blocking collectives, joined(): pieces = lax.all_gather(value, axis)  5.36 us
    another operation x8, other arithmetic, fold_slots(): states = jnp.stack([1.0 - detect_prob, detect_prob], axis=1)  3.81 us
    sub x8, other arithmetic, fold_slots(): states = jnp.stack([1.0 - detect_prob, detect_prob], axis=1)  2.91 us
  transfers between devices with their start and end apart: 15, of which 6 were waited for; matrix products, arithmetic and copies ran while one was open for 1% of the time, Pallas kernels for 0%

profile of v1, /device:TPU:11, one launch (start us, length us, event | category | flops | bytes accessed | tf_op | source)
XLA Modules:
  0.0 94.7 jit_solution(6734185073316448563)
XLA Ops:
  0.0 0.7 fusion.24
  0.8 0.8 select_reduce_fusion
  1.7 0.7 multiply_add_fusion.35
  2.3 0.8 convert_bitcast_fusion.1
  3.1 2.0 %convolution_convert_fusion = bf16[128,4096]{1,0:T(8,128)(2,1)S(1)} fusion(bf16[64,4096]{1,0:T(8,128)(2,1)} %param.11, f32[64]{0:T(128)S(1)} %get-tuple-element.148, f32[4096]{0:T(1024)S(1)} %get-tuple-element.150, f32[64]{0:T(128)S(1)} %get-tuple-element.147, f32[4096]{0:T(1024)S(1)} %get-tuple-element.149, f32[64]{0:T(128)} %param.9, ...), kind=kOutput, calls=%fused_computation.71 | convolution fusion | flops 71311360 | bytes 1606656 | tf_op jit(solution)/shard_map/dot_general | solution.py:117
  5.1 0.8 reshape.1052
  6.0 1.1 %constant_dynamic-slice_fusion.1 = (bf16[8,2,2048]{2,1,0:T(2,128)(2,1)S(1)}, bf16[8,2,2048]{2,1,0:T(2,128)(2,1)S(1)}, bf16[8,2,2048]{2,1,0:T(2,128)(2,1)S(1)}, b...) fusion(bf16[128,2,2048]{2,1,0:T(2,128)(2,1)S(1)} %reshape.1052,, ...), kind=kLoop, calls=%fused_computation.130 | loop fusion | bytes 2097216 | tf_op jit(solution)/shard_map/dynamic_slice | solution.py:20
  7.1 0.7 collective-permute-start
  7.9 1.3 %collective-permute-start.1 = (bf16[8,2,2048]{2,0,1:T(8,128)(2,1)S(1)}, bf16[8,2,2048]{2,0,1:T(8,128)(2,1)S(1)}, u32[]{:S(2)}, u32[]{:S(2)}) collective-permute-start(bf16[8,2,2048]{2,0,1:T(8,128)(2,1)S(1)} %copy.39), channel_id=1, source_target_pairs={{0,2},{1,3},{2,0},{3,1},{4,6},{5,7},{6,4},{7,5},{8,10},{9,11},{10,... | collective-permute-start | bytes 196616 | tf_op jit(solution)/shard_map/ppermute | solution.py:22
  9.2 0.5 collective-permute-start.2
  10.0 1.7 %collective-permute-start.4 = (bf16[8,2,2048]{2,0,1:T(8,128)(2,1)S(1)}, bf16[8,2,2048]{2,0,1:T(8,128)(2,1)S(1)}, u32[]{:S(2)}, u32[]{:S(2)}) collective-permute-start(bf16[8,2,2048]{2,0,1:T(8,128)(2,1)S(1)} %copy.42), channel_id=1, source_target_pairs={{0,5},{1,4},{2,7},{3,6},{4,1},{5,0},{6,3},{7,2},{8,13},{9,12},{10,... | collective-permute-start | bytes 196616 | tf_op jit(solution)/shard_map/ppermute | solution.py:22
  12.2 1.2 %collective-permute-start.5 = (bf16[8,2,2048]{2,0,1:T(8,128)(2,1)S(1)}, bf16[8,2,2048]{2,0,1:T(8,128)(2,1)S(1)}, u32[]{:S(2)}, u32[]{:S(2)}) collective-permute-start(bf16[8,2,2048]{2,0,1:T(8,128)(2,1)S(1)} %copy.43), channel_id=1, source_target_pairs={{0,6},{1,7},{2,4},{3,5},{4,2},{5,3},{6,0},{7,1},{8,14},{9,15},{10,... | collective-permute-start | bytes 196616 | tf_op jit(solution)/shard_map/ppermute | solution.py:22
  13.5 1.5 %collective-permute-start.6 = (bf16[8,2,2048]{2,0,1:T(8,128)(2,1)S(1)}, bf16[8,2,2048]{2,0,1:T(8,128)(2,1)S(1)}, u32[]{:S(2)}, u32[]{:S(2)}) collective-permute-start(bf16[8,2,2048]{2,0,1:T(8,128)(2,1)S(1)} %copy.44), channel_id=1, source_target_pairs={{0,7},{1,6},{2,5},{3,4},{4,3},{5,2},{6,1},{7,0},{8,15},{9,14},{10,... | collective-permute-start | bytes 196616 | tf_op jit(solution)/shard_map/ppermute | solution.py:22
  15.0 2.4 %collective-permute-start.7 = (bf16[8,2,2048]{2,0,1:T(8,128)(2,1)S(1)}, bf16[8,2,2048]{2,0,1:T(8,128)(2,1)S(1)}, u32[]{:S(2)}, u32[]{:S(2)}) collective-permute-start(bf16[8,2,2048]{2,0,1:T(8,128)(2,1)S(1)} %copy.45), channel_id=1, source_target_pairs={{0,8},{1,9},{2,10},{3,11},{4,12},{5,13},{6,14},{7,15},{8,0},{9,1},... | collective-permute-start | bytes 196616 | tf_op jit(solution)/shard_map/ppermute | solution.py:22
  17.4 0.5 collective-permute-start.8
  17.9 3.3 %collective-permute-start.9 = (bf16[8,2,2048]{2,0,1:T(8,128)(2,1)S(1)}, bf16[8,2,2048]{2,0,1:T(8,128)(2,1)S(1)}, u32[]{:S(2)}, u32[]{:S(2)}) collective-permute-start(bf16[8,2,2048]{2,0,1:T(8,128)(2,1)S(1)} %copy.47), channel_id=1, source_target_pairs={{0,10},{1,11},{2,8},{3,9},{4,14},{5,15},{6,12},{7,13},{8,2},{9,3},... | collective-permute-start | bytes 196616 | tf_op jit(solution)/shard_map/ppermute | solution.py:22
  21.6 1.4 %collective-permute-start.11 = (bf16[8,2,2048]{2,0,1:T(8,128)(2,1)S(1)}, bf16[8,2,2048]{2,0,1:T(8,128)(2,1)S(1)}, u32[]{:S(2)}, u32[]{:S(2)}) collective-permute-start(bf16[8,2,2048]{2,0,1:T(8,128)(2,1)S(1)} %copy.49), channel_id=1, source_target_pairs={{0,12},{1,13},{2,14},{3,15},{4,8},{5,9},{6,10},{7,11},{8,4},{9,5},... | collective-permute-start | bytes 196616 | tf_op jit(solution)/shard_map/ppermute | solution.py:22
  23.0 0.6 collective-permute-start.12
  23.5 3.9 %collective-permute-done.8 = bf16[8,2,2048]{2,0,1:T(8,128)(2,1)S(1)} collective-permute-done((bf16[8,2,2048]{2,0,1:T(8,128)(2,1)S(1)}, bf16[8,2,2048]{2,0,1:T(8,128)(2,1)S(1)}, u32[]{:S(2)}, u32[]{:S(2)}) %collective-permute-start.8) | collective-permute-done | bytes 65568 | tf_op jit(solution)/shard_map/ppermute | solution.py:22
  27.4 0.9 %collective-permute-start.13 = (bf16[8,2,2048]{2,0,1:T(8,128)(2,1)S(1)}, bf16[8,2,2048]{2,0,1:T(8,128)(2,1)S(1)}, u32[]{:S(2)}, u32[]{:S(2)}) collective-permute-start(bf16[8,2,2048]{2,0,1:T(8,128)(2,1)S(1)} %copy.51), channel_id=1, source_target_pairs={{0,14},{1,15},{2,12},{3,13},{4,10},{5,11},{6,8},{7,9},{8,6},{9,7},... | collective-permute-start | bytes 196616 | tf_op jit(solution)/shard_map/ppermute | solution.py:22
  28.4 0.6 collective-permute-done.9
  29.0 2.7 %collective-permute-start.14 = (bf16[8,2,2048]{2,0,1:T(8,128)(2,1)S(1)}, bf16[8,2,2048]{2,0,1:T(8,128)(2,1)S(1)}, u32[]{:S(2)}, u32[]{:S(2)}) collective-permute-start(bf16[8,2,2048]{2,0,1:T(8,128)(2,1)S(1)} %copy.52), channel_id=1, source_target_pairs={{0,15},{1,14},{2,13},{3,12},{4,11},{5,10},{6,9},{7,8},{8,7},{9,6},... | collective-permute-start | bytes 196616 | tf_op jit(solution)/shard_map/ppermute | solution.py:22
  31.7 2.9 %collective-permute-done.11 = bf16[8,2,2048]{2,0,1:T(8,128)(2,1)S(1)} collective-permute-done((bf16[8,2,2048]{2,0,1:T(8,128)(2,1)S(1)}, bf16[8,2,2048]{2,0,1:T(8,128)(2,1)S(1)}, u32[]{:S(2)}, u32[]{:S(2)}) %collective-permute-start.11) | collective-permute-done | bytes 65568 | tf_op jit(solution)/shard_map/ppermute | solution.py:22
  34.6 2.8 %collective-permute-done.12 = bf16[8,2,2048]{2,0,1:T(8,128)(2,1)S(1)} collective-permute-done((bf16[8,2,2048]{2,0,1:T(8,128)(2,1)S(1)}, bf16[8,2,2048]{2,0,1:T(8,128)(2,1)S(1)}, u32[]{:S(2)}, u32[]{:S(2)}) %collective-permute-start.12) | collective-permute-done | bytes 65568 | tf_op jit(solution)/shard_map/ppermute | solution.py:22
  37.4 3.1 %collective-permute-done.13 = bf16[8,2,2048]{2,0,1:T(8,128)(2,1)S(1)} collective-permute-done((bf16[8,2,2048]{2,0,1:T(8,128)(2,1)S(1)}, bf16[8,2,2048]{2,0,1:T(8,128)(2,1)S(1)}, u32[]{:S(2)}, u32[]{:S(2)}) %collective-permute-start.13) | collective-permute-done | bytes 65568 | tf_op jit(solution)/shard_map/ppermute | solution.py:22
  40.5 1.4 %collective-permute-done.14 = bf16[8,2,2048]{2,0,1:T(8,128)(2,1)S(1)} collective-permute-done((bf16[8,2,2048]{2,0,1:T(8,128)(2,1)S(1)}, bf16[8,2,2048]{2,0,1:T(8,128)(2,1)S(1)}, u32[]{:S(2)}, u32[]{:S(2)}) %collective-permute-start.14) | collective-permute-done | bytes 65568 | tf_op jit(solution)/shard_map/ppermute | solution.py:22
  41.9 45.9 %while.25 = (s32[]{:T(128)}, f32[2,8,2048]{2,1,0:T(8,128)S(1)}, bf16[2,128,2048]{2,1,0:T(8,128)(2,1)S(1)}, s32[]{:T(128)}, s32[]{:T(128)}, /*index=5*/s32[]{:T(128)}) while((s32[]{:T(128)}, f32[2,8,2048]{2,1,0:T(8,128)S(1)}, bf16[2,128,2048]{2,1,0:T(8,128)(2,1)S(1)}, s32[]{:T(128)}, s32[]{:T(128)}, /*index=5*/s32[]{:T(128)}) %tuple.154), condition=%wide.region_5.6_spmd, body=%wide.region_2.5_spmd.sunk | while | flops 1654788 | bytes 14295218 | solution.py:122
  42.4 22.5 %while.26 = (s32[]{:T(128)}, f32[4,8,512]{2,1,0:T(8,128)S(1)}, bf16[4,128,512]{2,0,1:T(4,128)(2,1)S(1)}, s32[]{:T(128)}) while((s32[]{:T(128)}, f32[4,8,512]{2,1,0:T(8,128)S(1)}, bf16[4,128,512]{2,0,1:T(4,128)(2,1)S(1)}, s32[]{:T(128)}) %tuple.153), condition=%wide.region_4.4_spmd, body=%wide.region_3.3_spmd.sunk | while | flops 1654786 | bytes 12066877 | solution.py:82
  42.8 0.5 pad_maximum_fusion.4
  44.5 0.5 stack.31
  48.4 0.5 pad_maximum_fusion.4
  50.1 0.5 stack.31
  54.0 0.5 pad_maximum_fusion.4
  55.7 0.5 stack.31
  59.6 0.5 pad_maximum_fusion.4
  61.3 0.5 stack.31
  62.6 0.4 stack.32
  65.3 22.5 %while.26 = (s32[]{:T(128)}, f32[4,8,512]{2,1,0:T(8,128)S(1)}, bf16[4,128,512]{2,0,1:T(4,128)(2,1)S(1)}, s32[]{:T(128)}) while((s32[]{:T(128)}, f32[4,8,512]{2,1,0:T(8,128)S(1)}, bf16[4,128,512]{2,0,1:T(4,128)(2,1)S(1)}, s32[]{:T(128)}) %tuple.153), condition=%wide.region_4.4_spmd, body=%wide.region_3.3_spmd.sunk | while | flops 1654786 | bytes 12066877 | solution.py:82
  65.7 0.5 pad_maximum_fusion.4
  67.4 0.5 stack.31
  71.3 0.5 pad_maximum_fusion.4
  73.0 0.5 stack.31
  76.9 0.5 pad_maximum_fusion.4
  78.6 0.5 stack.31
  82.5 0.5 pad_maximum_fusion.4
  84.2 0.5 stack.31
  87.8 5.4 %all-gather = f32[16,2,2048]{2,0,1:T(8,128)S(1)} all-gather(f32[8,2,2048]{2,0,1:T(8,128)S(1)} %bitcast.234), channel_id=2, replica_groups=mesh['grp'=2,'tile'=16] {'grp'}, dimensions={0}, use_global_device_ids=true | all-gather | bytes 393216 | tf_op jit(solution)/shard_map/all_gather | solution.py:28
  94.1 0.6 dynamic-slice_bitcast_fusion
  (330 shorter events, 37.3 us)
Async XLA Ops:
  7.1 5.1 %collective-permute-start = (bf16[8,2,2048]{2,0,1:T(8,128)(2,1)S(1)}, bf16[8,2,2048]{2,0,1:T(8,128)(2,1)S(1)}, u32[]{:S(2)}, u32[]{:S(2)}) collective-permute-start(bf16[8,2,2048]{2,0,1:T(8,128)(2,1)S(1)} %copy.38), channel_id=1, source_target_pairs={{0,1},{1,0},{2,3},{3,2},{4,5},{5,4},{6,7},{7,6},{8,9},{9,8},{10,11... | collective-permute-start | bytes 196616 | tf_op jit(solution)/shard_map/ppermute | solution.py:22
  7.9 5.5 %collective-permute-start.1 = (bf16[8,2,2048]{2,0,1:T(8,128)(2,1)S(1)}, bf16[8,2,2048]{2,0,1:T(8,128)(2,1)S(1)}, u32[]{:S(2)}, u32[]{:S(2)}) collective-permute-start(bf16[8,2,2048]{2,0,1:T(8,128)(2,1)S(1)} %copy.39), channel_id=1, source_target_pairs={{0,2},{1,3},{2,0},{3,1},{4,6},{5,7},{6,4},{7,5},{8,10},{9,11},{10,... | collective-permute-start | bytes 196616 | tf_op jit(solution)/shard_map/ppermute | solution.py:22
  9.2 5.7 %collective-permute-start.2 = (bf16[8,2,2048]{2,0,1:T(8,128)(2,1)S(1)}, bf16[8,2,2048]{2,0,1:T(8,128)(2,1)S(1)}, u32[]{:S(2)}, u32[]{:S(2)}) collective-permute-start(bf16[8,2,2048]{2,0,1:T(8,128)(2,1)S(1)} %copy.40), channel_id=1, source_target_pairs={{0,3},{1,2},{2,1},{3,0},{4,7},{5,6},{6,5},{7,4},{8,11},{9,10},{10,... | collective-permute-start | bytes 196616 | tf_op jit(solution)/shard_map/ppermute | solution.py:22
  9.7 7.6 %collective-permute-start.3 = (bf16[8,2,2048]{2,0,1:T(8,128)(2,1)S(1)}, bf16[8,2,2048]{2,0,1:T(8,128)(2,1)S(1)}, u32[]{:S(2)}, u32[]{:S(2)}) collective-permute-start(bf16[8,2,2048]{2,0,1:T(8,128)(2,1)S(1)} %copy.41), channel_id=1, source_target_pairs={{0,4},{1,5},{2,6},{3,7},{4,0},{5,1},{6,2},{7,3},{8,12},{9,13},{10,... | collective-permute-start | bytes 196616 | tf_op jit(solution)/shard_map/ppermute | solution.py:22
  10.0 7.9 %collective-permute-start.4 = (bf16[8,2,2048]{2,0,1:T(8,128)(2,1)S(1)}, bf16[8,2,2048]{2,0,1:T(8,128)(2,1)S(1)}, u32[]{:S(2)}, u32[]{:S(2)}) collective-permute-start(bf16[8,2,2048]{2,0,1:T(8,128)(2,1)S(1)} %copy.42), channel_id=1, source_target_pairs={{0,5},{1,4},{2,7},{3,6},{4,1},{5,0},{6,3},{7,2},{8,13},{9,12},{10,... | collective-permute-start | bytes 196616 | tf_op jit(solution)/shard_map/ppermute | solution.py:22
  12.2 9.0 %collective-permute-start.5 = (bf16[8,2,2048]{2,0,1:T(8,128)(2,1)S(1)}, bf16[8,2,2048]{2,0,1:T(8,128)(2,1)S(1)}, u32[]{:S(2)}, u32[]{:S(2)}) collective-permute-start(bf16[8,2,2048]{2,0,1:T(8,128)(2,1)S(1)} %copy.43), channel_id=1, source_target_pairs={{0,6},{1,7},{2,4},{3,5},{4,2},{5,3},{6,0},{7,1},{8,14},{9,15},{10,... | collective-permute-start | bytes 196616 | tf_op jit(solution)/shard_map/ppermute | solution.py:22
  13.5 8.1 %collective-permute-start.6 = (bf16[8,2,2048]{2,0,1:T(8,128)(2,1)S(1)}, bf16[8,2,2048]{2,0,1:T(8,128)(2,1)S(1)}, u32[]{:S(2)}, u32[]{:S(2)}) collective-permute-start(bf16[8,2,2048]{2,0,1:T(8,128)(2,1)S(1)} %copy.44), channel_id=1, source_target_pairs={{0,7},{1,6},{2,5},{3,4},{4,3},{5,2},{6,1},{7,0},{8,15},{9,14},{10,... | collective-permute-start | bytes 196616 | tf_op jit(solution)/shard_map/ppermute | solution.py:22
  15.0 8.0 %collective-permute-start.7 = (bf16[8,2,2048]{2,0,1:T(8,128)(2,1)S(1)}, bf16[8,2,2048]{2,0,1:T(8,128)(2,1)S(1)}, u32[]{:S(2)}, u32[]{:S(2)}) collective-permute-start(bf16[8,2,2048]{2,0,1:T(8,128)(2,1)S(1)} %copy.45), channel_id=1, source_target_pairs={{0,8},{1,9},{2,10},{3,11},{4,12},{5,13},{6,14},{7,15},{8,0},{9,1},... | collective-permute-start | bytes 196616 | tf_op jit(solution)/shard_map/ppermute | solution.py:22
  17.4 10.1 %collective-permute-start.8 = (bf16[8,2,2048]{2,0,1:T(8,128)(2,1)S(1)}, bf16[8,2,2048]{2,0,1:T(8,128)(2,1)S(1)}, u32[]{:S(2)}, u32[]{:S(2)}) collective-permute-start(bf16[8,2,2048]{2,0,1:T(8,128)(2,1)S(1)} %copy.46), channel_id=1, source_target_pairs={{0,9},{1,8},{2,11},{3,10},{4,13},{5,12},{6,15},{7,14},{8,1},{9,0},... | collective-permute-start | bytes 196616 | tf_op jit(solution)/shard_map/ppermute | solution.py:22
  17.9 11.1 %collective-permute-start.9 = (bf16[8,2,2048]{2,0,1:T(8,128)(2,1)S(1)}, bf16[8,2,2048]{2,0,1:T(8,128)(2,1)S(1)}, u32[]{:S(2)}, u32[]{:S(2)}) collective-permute-start(bf16[8,2,2048]{2,0,1:T(8,128)(2,1)S(1)} %copy.47), channel_id=1, source_target_pairs={{0,10},{1,11},{2,8},{3,9},{4,14},{5,15},{6,12},{7,13},{8,2},{9,3},... | collective-permute-start | bytes 196616 | tf_op jit(solution)/shard_map/ppermute | solution.py:22
  21.2 10.5 %collective-permute-start.10 = (bf16[8,2,2048]{2,0,1:T(8,128)(2,1)S(1)}, bf16[8,2,2048]{2,0,1:T(8,128)(2,1)S(1)}, u32[]{:S(2)}, u32[]{:S(2)}) collective-permute-start(bf16[8,2,2048]{2,0,1:T(8,128)(2,1)S(1)} %copy.48), channel_id=1, source_target_pairs={{0,11},{1,10},{2,9},{3,8},{4,15},{5,14},{6,13},{7,12},{8,3},{9,2},... | collective-permute-start | bytes 196616 | tf_op jit(solution)/shard_map/ppermute | solution.py:22
  21.6 13.1 %collective-permute-start.11 = (bf16[8,2,2048]{2,0,1:T(8,128)(2,1)S(1)}, bf16[8,2,2048]{2,0,1:T(8,128)(2,1)S(1)}, u32[]{:S(2)}, u32[]{:S(2)}) collective-permute-start(bf16[8,2,2048]{2,0,1:T(8,128)(2,1)S(1)} %copy.49), channel_id=1, source_target_pairs={{0,12},{1,13},{2,14},{3,15},{4,8},{5,9},{6,10},{7,11},{8,4},{9,5},... | collective-permute-start | bytes 196616 | tf_op jit(solution)/shard_map/ppermute | solution.py:22
  23.0 14.4 %collective-permute-start.12 = (bf16[8,2,2048]{2,0,1:T(8,128)(2,1)S(1)}, bf16[8,2,2048]{2,0,1:T(8,128)(2,1)S(1)}, u32[]{:S(2)}, u32[]{:S(2)}) collective-permute-start(bf16[8,2,2048]{2,0,1:T(8,128)(2,1)S(1)} %copy.50), channel_id=1, source_target_pairs={{0,13},{1,12},{2,15},{3,14},{4,9},{5,8},{6,11},{7,10},{8,5},{9,4},... | collective-permute-start | bytes 196616 | tf_op jit(solution)/shard_map/ppermute | solution.py:22
  27.4 13.1 %collective-permute-start.13 = (bf16[8,2,2048]{2,0,1:T(8,128)(2,1)S(1)}, bf16[8,2,2048]{2,0,1:T(8,128)(2,1)S(1)}, u32[]{:S(2)}, u32[]{:S(2)}) collective-permute-start(bf16[8,2,2048]{2,0,1:T(8,128)(2,1)S(1)} %copy.51), channel_id=1, source_target_pairs={{0,14},{1,15},{2,12},{3,13},{4,10},{5,11},{6,8},{7,9},{8,6},{9,7},... | collective-permute-start | bytes 196616 | tf_op jit(solution)/shard_map/ppermute | solution.py:22
  29.0 12.9 %collective-permute-start.14 = (bf16[8,2,2048]{2,0,1:T(8,128)(2,1)S(1)}, bf16[8,2,2048]{2,0,1:T(8,128)(2,1)S(1)}, u32[]{:S(2)}, u32[]{:S(2)}) collective-permute-start(bf16[8,2,2048]{2,0,1:T(8,128)(2,1)S(1)} %copy.52), channel_id=1, source_target_pairs={{0,15},{1,14},{2,13},{3,12},{4,11},{5,10},{6,9},{7,8},{8,7},{9,6},... | collective-permute-start | bytes 196616 | tf_op jit(solution)/shard_map/ppermute | solution.py:22
